TPU v7x, 512 devices: a whole 4x4x16 slice. The times are simulated.
512 devices in a mesh: dp: 128 (over z, y, core), shard: 4 (over x).
Axes of the slice: x: 4, y: 4, z: 16, core: 2. Of those that a mesh axis runs over, the one named last changes fastest.
Arguments:
- key_grad: bfloat16 [128, 512, 2560], P('dp', 'shard'), may hold values from -90 to 90
- key_error: float32 [128, 512, 2560], P('dp', 'shard'), may hold values from -4 to 4
- router_grad: bfloat16 [128, 64, 2560], P('dp', 'shard'), may hold values from -90 to 90
- router_error: float32 [128, 64, 2560], P('dp', 'shard'), may hold values from -4 to 4
- norm_grad: bfloat16 [128, 2, 2560], P('dp', None, 'shard'), may hold values from -8 to 8
- key_basis: float32 [32, 2560], replicated, may hold values from -6 to 6
- router_basis: float32 [32, 2560], replicated, may hold values from -6 to 6
- key_momentum: float32 [512, 2560], P('shard', 'dp'), may hold values from -4 to 4
- key_weight: float32 [512, 2560], P('shard', 'dp'), may hold values from -4 to 4
- router_momentum: float32 [64, 2560], P('shard', 'dp'), may hold values from -4 to 4
- router_weight: float32 [64, 2560], P('shard', 'dp'), may hold values from -4 to 4
- norm_momentum: float32 [2, 2560], P(None, 'shard'), may hold values from -4 to 4
- norm_weight: float32 [2, 2560], P(None, 'shard'), may hold values from 0.5 to 1.5
Outputs:
- key_carry: float32 [128, 512, 2560], P('dp', 'shard')
- router_carry: float32 [128, 64, 2560], P('dp', 'shard')
- key_velocity: float32 [512, 2560], P('shard', 'dp')
- key_master: float32 [512, 2560], P('shard', 'dp')
- key_params: bfloat16 [512, 2560], P(None, 'dp')
- router_velocity: float32 [64, 2560], P('shard', 'dp')
- router_master: float32 [64, 2560], P('shard', 'dp')
- router_params: bfloat16 [64, 2560], P(None, 'dp')
- norm_velocity: float32 [2, 2560], P(None, 'shard')
- norm_master: float32 [2, 2560], P(None, 'shard')
- norm_params: bfloat16 [2, 2560], replicated
All inputs are finite; a program needn't handle non-finite values.
Results may differ from a plain program's by a relative error of at most 0.008.
Values may be sent and summed in bfloat16 or wider, within the bound.
No kernel may reach another device: no remote copies, remote signals or barrier semaphores. Data moves between devices by JAX's collectives and lax.ppermute only.
A program may use at most 64 MiB of HBM per device.

v0:
```python
import jax
import jax.numpy as jnp
from jax import lax
from jax.sharding import PartitionSpec as P

ROOT_STEPS = 4
highest = lax.Precision.HIGHEST
momentum_decay = 0.9
learning_rate = 0.1


def inverse_root(gram_matrix):
    scaling = jnp.sqrt(jnp.sum(gram_matrix * gram_matrix)) + 1e-06
    identity = jnp.eye(gram_matrix.shape[0], dtype=jnp.float32)
    square_side = gram_matrix / scaling
    root_side = identity
    for sweep_index in range(ROOT_STEPS):
        middle = 1.5 * identity - 0.5 * jnp.dot(root_side, square_side, precision=highest)
        square_side = jnp.dot(square_side, middle, precision=highest)
        root_side = jnp.dot(middle, root_side, precision=highest)
    return (root_side, scaling)


def project(old_basis, merged):
    return lax.dot_general(old_basis, merged, (((1,), (1,)), ((), ())), precision=highest)


def gram_of(factor_rows):
    return lax.dot_general(factor_rows, factor_rows, (((1,), (1,)), ((), ())), precision=highest)


def normalize(gram_matrix, factor_rows):
    root_side, scaling = inverse_root(gram_matrix)
    return jnp.dot(root_side, factor_rows, precision=highest) / jnp.sqrt(scaling)


def advance(momentum, weight, direction):
    velocity = momentum_decay * momentum + direction
    return (velocity, weight - learning_rate * velocity)


def body(
    key_grad,
    key_error,
    router_grad,
    router_error,
    norm_grad,
    key_basis,
    router_basis,
    key_momentum,
    key_weight,
    router_momentum,
    router_weight,
    norm_momentum,
    norm_weight,
):
    replicas = lax.axis_size("dp")
    rank_size = key_basis.shape[0]
    merged_key = key_grad[0].astype(jnp.float32) + key_error[0]
    merged_router = router_grad[0].astype(jnp.float32) + router_error[0]
    rows_key, rows_router, norm_sum = lax.psum(
        (
            project(key_basis, merged_key),
            project(router_basis, merged_router),
            norm_grad[0].astype(jnp.float32),
        ),
        "dp",
    )
    gram_key, gram_router = lax.psum((gram_of(rows_key), gram_of(rows_router)), "shard")
    ortho_key = normalize(gram_key, rows_key)
    ortho_router = normalize(gram_router, rows_router)
    key_part = lax.dot_general(merged_key, ortho_key, (((0,), (1,)), ((), ())), precision=highest)
    router_part = lax.dot_general(
        merged_router, ortho_router, (((0,), (1,)), ((), ())), precision=highest
    )
    column_sum = lax.psum(jnp.concatenate([key_part, router_part], axis=1), ("dp", "shard"))
    columns = column_sum / replicas
    approx_key = lax.dot_general(
        ortho_key, columns[:, :rank_size], (((0,), (1,)), ((), ())), precision=highest
    )
    approx_router = lax.dot_general(
        ortho_router, columns[:, rank_size:], (((0,), (1,)), ((), ())), precision=highest
    )
    col_width = key_momentum.shape[1]
    offset = lax.axis_index("dp") * col_width
    key_velocity, key_master = advance(
        key_momentum, key_weight, lax.dynamic_slice_in_dim(approx_key, offset, col_width, 1)
    )
    router_velocity, router_master = advance(
        router_momentum,
        router_weight,
        lax.dynamic_slice_in_dim(approx_router, offset, col_width, 1),
    )
    norm_velocity, norm_master = advance(norm_momentum, norm_weight, norm_sum / replicas)
    key_params, router_params, norm_params = (
        lax.all_gather(key_master.astype(jnp.bfloat16), "shard", axis=0, tiled=True),
        lax.all_gather(router_master.astype(jnp.bfloat16), "shard", axis=0, tiled=True),
        lax.all_gather(norm_master.astype(jnp.bfloat16), "shard", axis=1, tiled=True),
    )
    key_carry = (merged_key - approx_key)[None]
    router_carry = (merged_router - approx_router)[None]
    return (
        key_carry,
        router_carry,
        key_velocity,
        key_master,
        key_params,
        router_velocity,
        router_master,
        router_params,
        norm_velocity,
        norm_master,
        norm_params,
    )


def solution(mesh):
    return jax.shard_map(
        body,
        mesh=mesh,
        in_specs=(
            P("dp", "shard", None),
            P("dp", "shard", None),
            P("dp", "shard", None),
            P("dp", "shard", None),
            P("dp", None, "shard"),
            P(),
            P(),
            P("shard", "dp"),
            P("shard", "dp"),
            P("shard", "dp"),
            P("shard", "dp"),
            P(None, "shard"),
            P(None, "shard"),
        ),
        out_specs=(
            P("dp", "shard", None),
            P("dp", "shard", None),
            P("shard", "dp"),
            P("shard", "dp"),
            P(None, "dp"),
            P("shard", "dp"),
            P("shard", "dp"),
            P(None, "dp"),
            P(None, "shard"),
            P(None, "shard"),
            P(),
        ),
        check_vma=False,
    )
```

profile of v0, /device:TPU:8, one launch (start us, length us, event | category | flops | bytes accessed | tf_op | source)
XLA Modules:
  0.0 1036.4 jit_solution(1657459035492836335)
XLA Ops:
  7.2 0.7 bitcast_convert_fusion
  8.0 1.4 convolution_bitcast_fusion
  9.5 2.9 fusion.5
  12.4 497.1 %all-reduce = (f32[32,128]{1,0:T(8,128)S(1)}, f32[32,16]{0,1:T(8,128)S(1)}, f32[2,640]{1,0:T(2,128)S(1)}) all-reduce(f32[32,128]{1,0:T(8,128)S(1)} %fusion.5, f32[32,16]{0,1:T(8,128)S(1)} %convolution_bitcast_fusion, f32[2,640]{1,0:T(2,128)S(1)} %bitcast_convert_fusion), channel_id=1, replica_groups=mesh['dp'=128,'shard'=4] {'dp'}, use_global_device_ids=true, to_apply=%region_0.0 | all-reduce | flops 5888 | bytes 47104 | tf_op jit(solution)/shard_map/psum | solution.py:61
  509.9 17.1 %all-reduce.1 = (f32[32,32]{1,0:T(8,128)S(1)}, f32[32,32]{1,0:T(8,128)S(1)}) all-reduce(f32[32,32]{1,0:T(8,128)S(1)} %fusion.31, f32[32,32]{1,0:T(8,128)S(1)} %fusion.37), channel_id=1, replica_groups=mesh['dp'=128,'shard'=4] {'shard'}, use_global_device_ids=true, to_apply=%region_1.0 | all-reduce | flops 2048 | bytes 16384 | tf_op jit(solution)/shard_map/psum | solution.py:69
  527.0 0.6 multiply_reduce_fusion
  532.5 0.9 fusion
  534.1 0.9 pad_maximum_fusion
  535.0 0.6 fusion.28
  535.6 11.8 %all_gather.11 = bf16[2,2560]{1,0:T(2,128)(2,1)S(1)} all-gather(bf16[2,640]{1,0:T(2,128)(2,1)S(1)} %get-tuple-element.27), channel_id=1, replica_groups=mesh['dp'=128,'shard'=4] {'shard'}, dimensions={1}, use_global_device_ids=true | all-gather | bytes 12800 | tf_op jit(solution)/shard_map/all_gather | solution.py:98
  547.6 445.8 %all-reduce.4.cloned.1.call-done = f32[2560,64]{0,1:T(8,128)} async-done(((f32[2560,64]{0,1:T(8,128)}), f32[2560,64]{0,1:T(8,128)}) %all-reduce.4.cloned.1.call-update) | async-done | bytes 655376 | tf_op jit(solution)/shard_map/psum | solution.py:76
  993.4 1.1 broadcast_multiply_fusion
  994.9 2.3 fusion.18
  997.2 0.7 fusion.23
  997.9 0.7 fusion.29
  998.6 12.0 %all_gather.10 = bf16[64,20]{1,0:T(8,128)(2,1)S(1)} all-gather(bf16[16,20]{1,0:T(8,128)(2,1)S(1)} %get-tuple-element.30), channel_id=1, replica_groups=mesh['dp'=128,'shard'=4] {'shard'}, dimensions={0}, use_global_device_ids=true | all-gather | bytes 3200 | tf_op jit(solution)/shard_map/all_gather | solution.py:97
  1010.6 0.7 copy.29
  1011.3 2.6 fusion.4
  1013.9 1.0 fusion.30
  1014.8 0.7 copy.27
  1015.5 0.7 copy.26
  1016.2 12.0 %all_gather.9 = bf16[512,20]{1,0:T(8,128)(2,1)S(1)} all-gather(bf16[128,20]{1,0:T(8,128)(2,1)S(1)} %get-tuple-element.33), channel_id=1, replica_groups=mesh['dp'=128,'shard'=4] {'shard'}, dimensions={0}, use_global_device_ids=true | all-gather | bytes 25600 | tf_op jit(solution)/shard_map/all_gather | solution.py:96
  1028.2 0.7 copy.28
  1028.9 0.6 copy.32
  (54 shorter events, 5.0 us)
Async XLA Ops:
  7.2 2.3 copy-start
  7.2 986.2 %all-reduce.4.cloned.1.call-start = ((), (), s32[]{:S(2)}) async-start(), calls=%async_computation | async-start | bytes 1310720 | tf_op jit(solution)/shard_map/psum | solution.py:76
  9.4 523.1 %copy-start.1 = (f32[1,128,2560]{2,1,0:T(8,128)S(1)}, f32[1,128,2560]{2,1,0:T(8,128)}, u32[]{:S(2)}) copy-start(f32[1,128,2560]{2,1,0:T(8,128)} %param.14) | copy-start | bytes 3932164
  9.5 523.1 %copy-start.2 = (bf16[1,128,2560]{2,1,0:T(8,128)(2,1)S(1)}, bf16[1,128,2560]{2,1,0:T(8,128)(2,1)}, u32[]{:S(2)}) copy-start(bf16[1,128,2560]{2,1,0:T(8,128)(2,1)} %param.13) | copy-start | bytes 1966084
  531.6 2.0 copy-start.3
  531.6 2.0 copy-start.4
  533.4 1.6 copy-start.9
  533.4 1.6 copy-start.10
  533.6 13.8 %copy-start.5 = (f32[128,20]{0,1:T(8,128)S(1)}, f32[128,20]{0,1:T(8,128)}, u32[]{:S(2)}) copy-start(f32[128,20]{0,1:T(8,128)} %param.20) | copy-start | bytes 30724
  533.6 13.9 %copy-start.6 = (f32[128,20]{0,1:T(8,128)S(1)}, f32[128,20]{0,1:T(8,128)}, u32[]{:S(2)}) copy-start(f32[128,20]{0,1:T(8,128)} %param.21) | copy-start | bytes 30724
  994.6 3.3 copy-start.7
  994.6 3.3 copy-start.8
Sparse Core Ops, SparseCore 0:
  535.1 458.2 all-reduce.3
where the time goes:
time: 1040 us
  blocking collectives  550 us (53%)
  waiting for transfers between devices  446 us (43%)
  between operations  15.8 us (2%)
  matrix products  12.1 us (1%)
    psum x1, blocking collectives, body(): lax.psum((project(key_basis, merged_key), project(router_basis, merged_ro...  497 us
    psum x1, waiting for transfers between devices, body(): lax.psum(jnp.concatenate([key_part, router_part], axis=1), ('dp', 'shard'))  446 us
  transfers between devices with their start and end apart: 1, of which 1 were waited for; matrix products, arithmetic and copies ran while one was open for 0% of the time, Pallas kernels for 0%

commit v1 on v0

--- a/solution.py
+++ b/solution.py
@@ -7,6 +7,11 @@
 highest = lax.Precision.HIGHEST
 momentum_decay = 0.9
 learning_rate = 0.1
+
+
+def by_each_axis(value, axis_one, axis_two):
+    partial = lax.psum(value, axis_one)
+    return lax.psum(partial, axis_two)
 
 
 def inverse_root(gram_matrix):
@@ -73,7 +78,7 @@
     router_part = lax.dot_general(
         merged_router, ortho_router, (((0,), (1,)), ((), ())), precision=highest
     )
-    column_sum = lax.psum(jnp.concatenate([key_part, router_part], axis=1), ("dp", "shard"))
+    column_sum = by_each_axis(jnp.concatenate([key_part, router_part], axis=1), "dp", "shard")
     columns = column_sum / replicas
     approx_key = lax.dot_general(
         ortho_key, columns[:, :rank_size], (((0,), (1,)), ((), ())), precision=highest

time: 1040 us -> 971 us (0.934)
  waiting for transfers between devices: 446 us -> 380 us
    psum x1 -> x2, waiting for transfers between devices: 446 us -> 380 us  [the longest x1 333 us: by_each_axis(): partial = lax.psum(value, axis_one)]
  transfers between devices with their start and end apart: 1 -> 2, of which waited for: 1 -> 2; matrix products, arithmetic and copies ran while one was open for 0% -> 0% of each run, Pallas kernels for 0% -> 0%
where the time goes in v1:
time: 971 us
  blocking collectives  550 us (57%)
  waiting for transfers between devices  380 us (39%)
  between operations  15.9 us (2%)
  matrix products  12.1 us (1%)
    psum x1, blocking collectives, body(): lax.psum((project(key_basis, merged_key), project(router_basis, merged_ro...  497 us
    psum x1, waiting for transfers between devices, by_each_axis(): partial = lax.psum(value, axis_one)  333 us
    psum x1, waiting for transfers between devices, by_each_axis(): return lax.psum(partial, axis_two)  47 us
  transfers between devices with their start and end apart: 2, of which 2 were waited for; matrix products, arithmetic and copies ran while one was open for 0% of the time, Pallas kernels for 0%

profile of v1, /device:TPU:8, one launch (start us, length us, event | category | flops | bytes accessed | tf_op | source)
XLA Modules:
  0.0 970.7 jit_solution(10527914500235261780)
XLA Ops:
  7.2 0.7 bitcast_convert_fusion
  8.0 1.4 convolution_bitcast_fusion
  9.5 2.9 fusion.5
  12.4 497.1 %all-reduce = (f32[32,128]{1,0:T(8,128)S(1)}, f32[32,16]{0,1:T(8,128)S(1)}, f32[2,640]{1,0:T(2,128)S(1)}) all-reduce(f32[32,128]{1,0:T(8,128)S(1)} %fusion.5, f32[32,16]{0,1:T(8,128)S(1)} %convolution_bitcast_fusion, f32[2,640]{1,0:T(2,128)S(1)} %bitcast_convert_fusion), channel_id=1, replica_groups=mesh['dp'=128,'shard'=4] {'dp'}, use_global_device_ids=true, to_apply=%region_0.0 | all-reduce | flops 5888 | bytes 47104 | tf_op jit(solution)/shard_map/psum | solution.py:66
  509.9 17.1 %all-reduce.1 = (f32[32,32]{1,0:T(8,128)S(1)}, f32[32,32]{1,0:T(8,128)S(1)}) all-reduce(f32[32,32]{1,0:T(8,128)S(1)} %fusion.31, f32[32,32]{1,0:T(8,128)S(1)} %fusion.37), channel_id=1, replica_groups=mesh['dp'=128,'shard'=4] {'shard'}, use_global_device_ids=true, to_apply=%region_1.0 | all-reduce | flops 2048 | bytes 16384 | tf_op jit(solution)/shard_map/psum | solution.py:74
  527.0 0.6 multiply_reduce_fusion
  532.5 0.9 fusion
  534.1 0.9 pad_maximum_fusion
  535.1 332.9 %all-reduce.5.cloned.1.call-done = f32[2560,64]{0,1:T(8,128)} async-done(((f32[2560,64]{0,1:T(8,128)}), f32[2560,64]{0,1:T(8,128)}) %all-reduce.5.cloned.1.call-update) | async-done | bytes 655376 | tf_op jit(solution)/shard_map/psum | solution.py:13
  868.1 0.6 fusion.28
  868.7 12.1 %all_gather.11 = bf16[2,2560]{1,0:T(2,128)(2,1)S(1)} all-gather(bf16[2,640]{1,0:T(2,128)(2,1)S(1)} %get-tuple-element.27), channel_id=1, replica_groups=mesh['dp'=128,'shard'=4] {'shard'}, dimensions={1}, use_global_device_ids=true | all-gather | bytes 12800 | tf_op jit(solution)/shard_map/all_gather | solution.py:103
  880.9 47.0 %all-reduce.7.cloned.1.call-done = f32[2560,64]{0,1:T(8,128)} async-done(((f32[2560,64]{0,1:T(8,128)}), f32[2560,64]{0,1:T(8,128)}) %all-reduce.7.cloned.1.call-update) | async-done | bytes 655376 | tf_op jit(solution)/shard_map/psum | solution.py:14
  927.9 1.1 broadcast_multiply_fusion
  929.4 2.3 fusion.18
  931.7 0.7 fusion.23
  932.4 0.7 fusion.29
  933.1 11.9 %all_gather.10 = bf16[64,20]{1,0:T(8,128)(2,1)S(1)} all-gather(bf16[16,20]{1,0:T(8,128)(2,1)S(1)} %get-tuple-element.30), channel_id=1, replica_groups=mesh['dp'=128,'shard'=4] {'shard'}, dimensions={0}, use_global_device_ids=true | all-gather | bytes 3200 | tf_op jit(solution)/shard_map/all_gather | solution.py:102
  945.0 0.7 copy.29
  945.7 2.6 fusion.4
  948.2 1.0 fusion.30
  949.2 0.7 copy.27
  949.9 0.7 copy.26
  950.6 12.0 %all_gather.9 = bf16[512,20]{1,0:T(8,128)(2,1)S(1)} all-gather(bf16[128,20]{1,0:T(8,128)(2,1)S(1)} %get-tuple-element.33), channel_id=1, replica_groups=mesh['dp'=128,'shard'=4] {'shard'}, dimensions={0}, use_global_device_ids=true | all-gather | bytes 25600 | tf_op jit(solution)/shard_map/all_gather | solution.py:101
  962.6 0.7 copy.28
  (57 shorter events, 5.6 us)
Async XLA Ops:
  7.2 2.3 copy-start
  7.2 860.8 %all-reduce.5.cloned.1.call-start = ((), (), s32[]{:S(2)}) async-start(), calls=%async_computation | async-start | bytes 1310720 | tf_op jit(solution)/shard_map/psum | solution.py:13
  9.4 523.1 %copy-start.1 = (f32[1,128,2560]{2,1,0:T(8,128)S(1)}, f32[1,128,2560]{2,1,0:T(8,128)}, u32[]{:S(2)}) copy-start(f32[1,128,2560]{2,1,0:T(8,128)} %param.14) | copy-start | bytes 3932164
  9.5 523.1 %copy-start.2 = (bf16[1,128,2560]{2,1,0:T(8,128)(2,1)S(1)}, bf16[1,128,2560]{2,1,0:T(8,128)(2,1)}, u32[]{:S(2)}) copy-start(bf16[1,128,2560]{2,1,0:T(8,128)(2,1)} %param.13) | copy-start | bytes 1966084
  531.6 2.0 copy-start.3
  531.6 2.0 copy-start.4
  534.1 334.0 %copy-start.9 = (f32[2,640]{1,0:T(2,128)S(1)}, f32[2,640]{1,0:T(2,128)}, u32[]{:S(2)}) copy-start(f32[2,640]{1,0:T(2,128)} %param.25) | copy-start | bytes 15364
  534.1 334.0 %copy-start.10 = (f32[2,640]{1,0:T(2,128)S(1)}, f32[2,640]{1,0:T(2,128)}, u32[]{:S(2)}) copy-start(f32[2,640]{1,0:T(2,128)} %param.24) | copy-start | bytes 15364
  534.1 346.6 %copy-start.5 = (f32[128,20]{0,1:T(8,128)S(1)}, f32[128,20]{0,1:T(8,128)}, u32[]{:S(2)}) copy-start(f32[128,20]{0,1:T(8,128)} %param.20) | copy-start | bytes 30724
  534.1 346.7 %copy-start.6 = (f32[128,20]{0,1:T(8,128)S(1)}, f32[128,20]{0,1:T(8,128)}, u32[]{:S(2)}) copy-start(f32[128,20]{0,1:T(8,128)} %param.21) | copy-start | bytes 30724
  535.0 392.9 %all-reduce.7.cloned.1.call-start = ((), (), s32[]{:S(2)}) async-start(), calls=%async_computation.1 | async-start | bytes 1310720 | tf_op jit(solution)/shard_map/psum | solution.py:14
  929.1 3.3 copy-start.7
  929.1 3.3 copy-start.8
Sparse Core Ops, SparseCore 0:
  535.1 332.8 all-reduce.4
  870.5 57.3 all-reduce.6
